TPU v7x, 256 devices: a whole 4x4x8 slice. The times are simulated.
256 devices in a mesh: leaf: 16 (over y, x), sep: 8 (over z), mode: 2 (over core).
Axes of the slice: x: 4, y: 4, z: 8, core: 2. Of those that a mesh axis runs over, the one named last changes fastest.
Arguments:
- modes: bfloat16 [1024, 2048, 256], P(('leaf', 'sep'), 'mode'), may hold values from -0.125 to 0.125
- coupling: bfloat16 [1024, 2048, 256], P(('leaf', 'sep'), 'mode'), may hold values from -6 to 6
- eigenvalues: float32 [1024, 256], P(('leaf', 'sep'), 'mode'), may hold values from 200 to 4000
- separator_of: int32 [1024, 1], P(('leaf', 'sep')), may hold values from 0 to 7; in each aligned block of 8 rows (0 to 7, 8 to 15, ...) at most 2 rows name the same one
- row_offset: int32 [1024], P(('leaf', 'sep')), may hold values from 0 to 256
- stiffness: bfloat16 [8, 512, 512], P('sep', None, ('leaf', 'mode')), may hold values from -1 to 40
- start_block: bfloat16 [8, 512, 256], P('sep', ('leaf', 'mode')), may hold values from -40 to 40
- rotations: bfloat16 [8, 2, 256, 256], P('sep'), may hold values from -0.375 to 0.375
Outputs:
- subspace: bfloat16 [8, 512, 256], P('sep', ('leaf', 'mode'))
- column_norms: float32 [8, 2, 256], P('sep')
Inputs may be any that keep to these rules, and one draw needn't show every extreme that they name: `separator_of`: among the 8 leaves of one device at most 2 couple to one separator, and in every draw some separator gets exactly 2 of them.
All inputs are finite; a program needn't handle non-finite values.
Results may differ from a plain program's by a relative error of at most 0.0075.
Values may be sent and summed in bfloat16 or wider, within the bound.
No kernel may reach another device: no remote copies, remote signals or barrier semaphores. Data moves between devices by JAX's collectives and lax.ppermute only.
A program may use at most 64 MiB of HBM per device.

v0:
```python
import jax
import jax.numpy as jnp
from jax import lax
from jax.sharding import PartitionSpec as P

SEP_ROWS = 512
CAP = 2
ITERS = 2
epsilon = 1e-06


def leaf_projection(modes, coupling, eigenvalues):
    summed = lax.psum_scatter(
        jnp.einsum("ldm,ldw->mlw", modes, coupling, preferred_element_type=jnp.float32),
        "mode",
        scatter_dimension=0,
        tiled=True,
    )
    return (summed / jnp.sqrt(eigenvalues.T)[:, :, None]).astype(jnp.bfloat16)


def route_blocks(scaled, separator_of, row_offset):
    groups = lax.axis_size("sep")
    leaves = scaled.shape[1]
    target = separator_of[:, 0]
    leaf_order = jnp.arange(leaves)
    earlier = (target[:, None] == target[None, :]) & (leaf_order[None, :] < leaf_order[:, None])
    position = jnp.sum(earlier.astype(jnp.int32), 1)
    slot_of = target * CAP + position
    slot_table = slot_of[None, :] == jnp.arange(groups * CAP)[:, None]
    send_blocks = jnp.einsum(
        "sl,mlw->smw", slot_table.astype(jnp.bfloat16), scaled, preferred_element_type=jnp.float32
    ).astype(jnp.bfloat16)
    send_offsets = jnp.sum(jnp.where(slot_table, row_offset[None, :], 0), 1)
    block_shape = (groups, CAP, send_blocks.shape[1], send_blocks.shape[2])
    got_blocks, got_offsets = (
        lax.all_to_all(
            send_blocks.reshape(block_shape), "sep", split_axis=0, concat_axis=0, tiled=True
        ),
        lax.all_to_all(
            send_offsets.reshape(groups, CAP), "sep", split_axis=0, concat_axis=0, tiled=True
        ),
    )
    return (
        got_blocks.reshape(groups * CAP, block_shape[2], block_shape[3]),
        got_offsets.reshape(groups * CAP),
    )


def coupled_correction(full_block, blocks, offsets):
    width_rows = blocks.shape[2]

    def add_slot(slot_index, accumulated):
        offset = offsets[slot_index]
        weights = blocks[slot_index]
        window = lax.dynamic_slice_in_dim(full_block, offset, width_rows, 0)
        projected = jnp.dot(weights, window, preferred_element_type=jnp.float32).astype(
            jnp.bfloat16
        )
        update = jnp.einsum("mw,mc->wc", weights, projected, preferred_element_type=jnp.float32)
        current = lax.dynamic_slice_in_dim(accumulated, offset, width_rows, 0)
        return lax.dynamic_update_slice_in_dim(accumulated, current + update, offset, 0)

    initial = jnp.zeros(full_block.shape, jnp.float32)
    return lax.fori_loop(0, blocks.shape[0], add_slot, initial)


def gather_rows(own_block):
    return lax.all_gather(own_block, ("leaf", "mode"), axis=0, tiled=True)


def per_device(
    modes, coupling, eigenvalues, separator_of, row_offset, stiffness, start_block, rotations
):
    scaled = leaf_projection(modes, coupling, eigenvalues)
    blocks, offsets = route_blocks(scaled, separator_of, row_offset)
    stiff_columns = stiffness[0]
    own_block = start_block[0]
    ritz_turns = rotations[0]
    own_rows = own_block.shape[0]
    norm_list = []
    for iteration in range(ITERS):
        full_block = gather_rows(own_block)
        correction = coupled_correction(full_block, blocks, offsets)

        def assemble_rows(first_row, row_count, block_now=own_block, correction_now=correction):
            product = jnp.dot(stiff_columns, block_now, preferred_element_type=jnp.float32)
            return product - correction_now

        summed = lax.psum_scatter(
            assemble_rows(jnp.int32(0), lax.axis_size(("leaf", "mode")) * own_rows),
            ("leaf", "mode"),
            scatter_dimension=0,
            tiled=True,
        )
        squares = lax.psum(jnp.sum(summed * summed, 0), ("leaf", "mode"))
        column_scale = jnp.sqrt(squares / SEP_ROWS + epsilon)
        normed = (summed / column_scale).astype(jnp.bfloat16)
        own_block = jnp.dot(
            normed, ritz_turns[iteration], preferred_element_type=jnp.float32
        ).astype(jnp.bfloat16)
        norm_list.append(column_scale)
    return (own_block[None], jnp.stack(norm_list)[None])


def solution(mesh):
    in_specs = (
        P(("leaf", "sep"), "mode", None),
        P(("leaf", "sep"), "mode", None),
        P(("leaf", "sep"), "mode"),
        P(("leaf", "sep"), None),
        P(("leaf", "sep")),
        P("sep", None, ("leaf", "mode")),
        P("sep", ("leaf", "mode"), None),
        P("sep", None, None, None),
    )
    out_specs = (P("sep", ("leaf", "mode"), None), P("sep", None, None))
    return jax.shard_map(
        per_device, mesh=mesh, in_specs=in_specs, out_specs=out_specs, check_vma=False
    )
```

profile of v0, /device:TPU:1, one launch (start us, length us, event | category | flops | bytes accessed | tf_op | source)
XLA Modules:
  0.0 560.8 jit_solution(13401757239637969915)
XLA Ops:
  7.3 6.2 %convolution_bitcast_fusion = f32[256,8,256]{0,2,1:T(8,128)} fusion(bf16[8,1024,256]{2,1,0:T(8,128)(2,1)} %param.13, bf16[8,1024,256]{2,1,0:T(8,128)(2,1)} %param.12), kind=kOutput, calls=%fused_computation.13 | convolution fusion | flops 1073741824 | bytes 10485760 | tf_op jit(solution)/shard_map/ldm,ldw->mlw/dot_general | solution.py:14
  14.5 9.0 %all-to-all-start = ((s32[8,1,2]{2,1,0:T(1,128)}), s32[8,1,2]{2,1,0:T(1,128)S(1)}, u32[]{:S(2)}, u32[]{:S(2)}) async-start(s32[8,1,2]{2,1,0:T(1,128)} %bitcast.7), calls=%async_computation | async-start | bytes 8192 | tf_op jit(solution)/shard_map/all_to_all | solution.py:40
  23.5 9.3 %reduce-scatter.6.cloned.1.call-done = f32[128,8,256]{0,2,1:T(8,128)} async-done(((f32[256,8,256]{0,2,1:T(8,128)}), f32[128,8,256]{0,2,1:T(8,128)}) %reduce-scatter.6.cloned.1.call-update) | async-done | bytes 1048592 | tf_op jit(solution)/shard_map/reduce_scatter | solution.py:13
  37.3 6.8 %all-to-all-start.1 = ((bf16[8,2,128,256]{3,1,2,0:T(2,128)(2,1)}), bf16[8,2,128,256]{3,1,2,0:T(2,128)(2,1)S(1)}, u32[]{:S(2)}, u32[]{:S(2)}) async-start(bf16[8,2,128,256]{3,1,2,0:T(2,128)(2,1)} %copy.30), calls=%async_computation.2 | async-start | bytes 2097152 | tf_op jit(solution)/shard_map/all_to_all | solution.py:37
  44.2 25.3 %all-gather = bf16[1,512,256]{2,1,0:T(8,128)(2,1)S(1)} all-gather(bf16[1,16,256]{2,1,0:T(8,128)(2,1)S(1)} %copy-done.1), channel_id=2, replica_groups=mesh['leaf'=16,'sep'=8,'mode'=2] {'leaf','mode'}, dimensions={1}, use_global_device_ids=true | all-gather | bytes 270336 | tf_op jit(solution)/shard_map/all_gather | solution.py:69
  70.8 2.6 all-to-all-done.1
  73.6 74.0 %while.26 = (s32[]{:T(128)}, f32[512,256]{1,0:T(8,128)S(1)}, s32[16]{0:T(128)S(1)}, bf16[16,128,256]{2,1,0:T(8,128)(2,1)S(1)}, bf16[512,256]{1,0:T(8,128)(2,1)S(1)}, /*index=5*/s32[]{:T(128)}, s32[]{:T(128)}, s32[]{:T(128)}) while((s32[]{:T(128)}, f32[512,256]{1,0:T(8,128)S(1)}, s32[16]{0:T(128)S(1)}, bf16[16,128,256]{2,1,0:T(8,128)(2,1)S(1)}, ...), condition=%wide.region_4.5_spmd, body=%wide.region_3.4_spmd.sunk | while | flops 33652740 | bytes 1312903 | solution.py:65
  80.6 1.9 dynamic_update_slice.16
  85.4 1.9 dynamic_update_slice.16
  90.2 1.9 dynamic_update_slice.16
  99.3 1.9 dynamic_update_slice.16
  108.9 1.9 dynamic_update_slice.16
  117.8 1.9 dynamic_update_slice.16
  127.4 1.9 dynamic_update_slice.16
  148.8 80.6 %reduce-scatter.8.cloned.1.call-done = f32[16,256]{1,0:T(8,128)} async-done(((f32[512,256]{1,0:T(8,128)}), f32[16,256]{1,0:T(8,128)}) %reduce-scatter.8.cloned.1.call-update) | async-done | bytes 16400 | tf_op jit(solution)/shard_map/reduce_scatter | solution.py:90
  230.1 64.6 %psum.14 = f32[256]{0:T(256)S(1)} all-reduce(f32[256]{0:T(256)S(1)} %multiply_reduce_fusion.1), channel_id=1, replica_groups=mesh['leaf'=16,'sep'=8,'mode'=2] {'leaf','mode'}, use_global_device_ids=true, to_apply=%region_7.8 | all-reduce | flops 256 | bytes 2048 | tf_op jit(solution)/shard_map/psum | solution.py:96
  295.6 22.6 %all_gather.7 = bf16[512,256]{1,0:T(8,128)(2,1)S(1)} all-gather(bf16[16,256]{1,0:T(8,128)(2,1)S(1)} %convolution_convert_fusion.4), channel_id=1, replica_groups=mesh['leaf'=16,'sep'=8,'mode'=2] {'leaf','mode'}, dimensions={0}, use_global_device_ids=true | all-gather | bytes 270336 | tf_op jit(solution)/shard_map/all_gather | solution.py:69
  318.3 85.1 %while.27 = (s32[]{:T(128)}, f32[512,256]{0,1:T(8,128)S(1)}, s32[16]{0:T(128)S(1)}, bf16[16,128,256]{2,1,0:T(8,128)(2,1)S(1)}, bf16[512,256]{1,0:T(8,128)(2,1)S(1)}, /*index=5*/s32[]{:T(128)}, s32[]{:T(128)}, s32[]{:T(128)}) while((s32[]{:T(128)}, f32[512,256]{0,1:T(8,128)S(1)}, s32[16]{0:T(128)S(1)}, bf16[16,128,256]{2,1,0:T(8,128)(2,1)S(1)}, ...), condition=%wide.region_9.10_spmd, body=%wide.region_8.9_spmd.sunk | while | flops 33652740 | bytes 2884751 | solution.py:65
  326.8 1.9 dynamic_update_slice.17
  332.1 1.9 dynamic_update_slice.17
  337.4 1.9 dynamic_update_slice.17
  347.9 1.9 dynamic_update_slice.17
  353.1 2.2 dynamic_update_slice.17
  358.7 1.9 dynamic_update_slice.17
  369.2 1.9 dynamic_update_slice.17
  374.5 2.2 dynamic_update_slice.17
  380.1 1.9 dynamic_update_slice.17
  390.6 1.9 dynamic_update_slice.17
  395.8 2.2 dynamic_update_slice.17
  401.4 1.9 dynamic_update_slice.17
  404.7 82.7 %reduce-scatter.10.cloned.1.call-done = f32[16,256]{1,0:T(8,128)} async-done(((f32[512,256]{1,0:T(8,128)}), f32[16,256]{1,0:T(8,128)}) %reduce-scatter.10.cloned.1.call-update) | async-done | bytes 16400
  488.2 64.6 %psum.15 = f32[256]{0:T(256)S(1)} all-reduce(f32[256]{0:T(256)S(1)} %multiply_reduce_fusion), channel_id=1, replica_groups=mesh['leaf'=16,'sep'=8,'mode'=2] {'leaf','mode'}, use_global_device_ids=true, to_apply=%region_12.13 | all-reduce | flops 256 | bytes 2048 | tf_op jit(solution)/shard_map/psum | solution.py:96
  (171 shorter events, 71.8 us)
Async XLA Ops:
  7.2 140.5 %copy-start = (bf16[1,512,16]{1,2,0:T(8,128)(2,1)S(1)}, bf16[1,512,16]{1,2,0:T(8,128)(2,1)}, u32[]{:S(2)}) copy-start(bf16[1,512,16]{1,2,0:T(8,128)(2,1)} %param.17) | copy-start | bytes 49156
  7.2 6.3 %copy-start.4 = (s32[8,1]{0,1:T(1,128)S(1)}, s32[8,1]{0,1:T(1,128)}, u32[]{:S(2)}) copy-start(s32[8,1]{0,1:T(1,128)} %param.15) | copy-start | bytes 100
  7.2 6.5 %copy-start.5 = (s32[8]{0:T(128)S(1)}, s32[8]{0:T(128)}, u32[]{:S(2)}) copy-start(s32[8]{0:T(128)} %param.16) | copy-start | bytes 100
  7.2 16.3 %copy-start.2 = (f32[8,128]{1,0:T(8,128)S(1)}, f32[8,128]{1,0:T(8,128)}, u32[]{:S(2)}) copy-start(f32[8,128]{1,0:T(8,128)} %param.14) | copy-start | bytes 12292
  7.2 25.6 %reduce-scatter.6.cloned.1.call-start = ((), (), s32[]{:S(2)}) async-start(), calls=%async_computation.5 | async-start | bytes 3145728 | tf_op jit(solution)/shard_map/reduce_scatter | solution.py:13
  14.5 22.9 %all-to-all-start = ((s32[8,1,2]{2,1,0:T(1,128)}), s32[8,1,2]{2,1,0:T(1,128)S(1)}, u32[]{:S(2)}, u32[]{:S(2)}) async-start(s32[8,1,2]{2,1,0:T(1,128)} %bitcast.7), calls=%async_computation | async-start | bytes 8192 | tf_op jit(solution)/shard_map/all_to_all | solution.py:40
  34.5 9.6 %copy-start.1 = (bf16[1,16,256]{2,1,0:T(8,128)(2,1)S(1)}, bf16[1,16,256]{2,1,0:T(8,128)(2,1)}, u32[]{:S(2)}) copy-start(bf16[1,16,256]{2,1,0:T(8,128)(2,1)} %param.18) | copy-start | bytes 24580
  37.3 36.0 %all-to-all-start.1 = ((bf16[8,2,128,256]{3,1,2,0:T(2,128)(2,1)}), bf16[8,2,128,256]{3,1,2,0:T(2,128)(2,1)S(1)}, u32[]{:S(2)}, u32[]{:S(2)}) async-start(bf16[8,2,128,256]{3,1,2,0:T(2,128)(2,1)} %copy.30), calls=%async_computation.2 | async-start | bytes 2097152 | tf_op jit(solution)/shard_map/all_to_all | solution.py:37
  44.1 185.3 %reduce-scatter.8.cloned.1.call-start = ((), (), s32[]{:S(2)}) async-start(), calls=%async_computation.6 | async-start | bytes 540672 | tf_op jit(solution)/shard_map/reduce_scatter | solution.py:90
  73.6 221.1 %copy-start.3 = (bf16[1,2,256,256]{3,2,1,0:T(8,128)(2,1)S(1)}, bf16[1,2,256,256]{3,2,1,0:T(8,128)(2,1)}, u32[]{:S(2)}) copy-start(bf16[1,2,256,256]{3,2,1,0:T(8,128)(2,1)} %param.19) | copy-start | bytes 786436
  148.7 338.6 %reduce-scatter.10.cloned.1.call-start = ((), (), s32[]{:S(2)}) async-start(), calls=%async_computation.7 | async-start | bytes 540672
Sparse Core Ops, SparseCore 0:
  13.6 19.1 reduce-scatter.5
  148.9 80.5 reduce-scatter.7
  404.8 82.4 reduce-scatter.9
where the time goes:
time: 562 us; the launch traced here: 561 us
  blocking collectives  177 us (31%)
  waiting for transfers between devices  175 us (31%)
  local copies, waits for them, and re-layouts  89.7 us (16%)
  loops' own time  63.5 us (11%)
  matrix products  21.7 us (4%)
  starting transfers between devices  15.9 us (3%)
  between operations  13.9 us (2%)
    psum x2, blocking collectives, per_device(): squares = lax.psum(jnp.sum(summed * summed, 0), ('leaf', 'mode'))  129 us
    unnamed x4, waiting for transfers between devices  82.7 us
    reduce_scatter x1, waiting for transfers between devices, per_device(): lax.psum_scatter(assemble_rows(jnp.int32(0), lax.axis_size(('leaf', 'mode...  80.6 us
    another operation x2, loops' own time, coupled_correction(): return lax.fori_loop(0, blocks.shape[0], add_slot, initial)  63.5 us
    dynamic_update_slice x48, local copies, waits for them, and re-layouts, add_slot(): lax.dynamic_update_slice_in_dim(accumulated, current + update, offset, 0)  60.6 us
    all_gather x2, blocking collectives, gather_rows(): return lax.all_gather(own_block, ('leaf', 'mode'), axis=0, tiled=True)  48 us
    dynamic_slice x32, local copies, waits for them, and re-layouts, add_slot(): offset = offsets[slot_index]  18.8 us
    dot_general x32, matrix products, add_slot(): jnp.einsum('mw,mc->wc', weights, projected, preferred_element_type=jnp.fl...  11.9 us
  transfers between devices with their start and end apart: 5, of which 4 were waited for; matrix products, arithmetic and copies ran while one was open for 1% of the time, Pallas kernels for 0%

commit v1 on v0

--- a/solution.py
+++ b/solution.py
@@ -93,7 +93,8 @@
             scatter_dimension=0,
             tiled=True,
         )
-        squares = lax.psum(jnp.sum(summed * summed, 0), ("leaf", "mode"))
+        half = lax.psum(jnp.sum(summed * summed, 0), "leaf")
+        squares = lax.psum(half, "mode")
         column_scale = jnp.sqrt(squares / SEP_ROWS + epsilon)
         normed = (summed / column_scale).astype(jnp.bfloat16)
         own_block = jnp.dot(

time: 562 us -> 518 us (0.922)
  blocking collectives: 177 us -> 133 us
    psum x2 -> x4, blocking collectives: 129 us -> 85.5 us  [the longest x2 61.8 us: per_device(): half = lax.psum(jnp.sum(summed * summed, 0), 'leaf')]
where the time goes in v1:
time: 518 us; the launch traced here: 517 us
  waiting for transfers between devices  175 us (34%)
  blocking collectives  133 us (26%)
  local copies, waits for them, and re-layouts  89.7 us (17%)
  loops' own time  63.5 us (12%)
  matrix products  21.7 us (4%)
  starting transfers between devices  15.9 us (3%)
  between operations  13.9 us (3%)
    unnamed x4, waiting for transfers between devices  82.7 us
    reduce_scatter x1, waiting for transfers between devices, per_device(): lax.psum_scatter(assemble_rows(jnp.int32(0), lax.axis_size(('leaf', 'mode...  80.6 us
    another operation x2, loops' own time, coupled_correction(): return lax.fori_loop(0, blocks.shape[0], add_slot, initial)  63.5 us
    psum x2, blocking collectives, per_device(): half = lax.psum(jnp.sum(summed * summed, 0), 'leaf')  61.8 us
    dynamic_update_slice x48, local copies, waits for them, and re-layouts, add_slot(): lax.dynamic_update_slice_in_dim(accumulated, current + update, offset, 0)  60.6 us
    all_gather x2, blocking collectives, gather_rows(): return lax.all_gather(own_block, ('leaf', 'mode'), axis=0, tiled=True)  47.5 us
    psum x2, blocking collectives, per_device(): squares = lax.psum(half, 'mode')  23.7 us
    dynamic_slice x32, local copies, waits for them, and re-layouts, add_slot(): offset = offsets[slot_index]  18.8 us
  transfers between devices with their start and end apart: 5, of which 4 were waited for; matrix products, arithmetic and copies ran while one was open for 1% of the time, Pallas kernels for 0%

profile of v1, /device:TPU:1, one launch (start us, length us, event | category | flops | bytes accessed | tf_op | source)
XLA Modules:
  0.0 516.6 jit_solution(5746448079535010161)
XLA Ops:
  7.3 6.2 %convolution_bitcast_fusion = f32[256,8,256]{0,2,1:T(8,128)} fusion(bf16[8,1024,256]{2,1,0:T(8,128)(2,1)} %param.13, bf16[8,1024,256]{2,1,0:T(8,128)(2,1)} %param.12), kind=kOutput, calls=%fused_computation.13 | convolution fusion | flops 1073741824 | bytes 10485760 | tf_op jit(solution)/shard_map/ldm,ldw->mlw/dot_general | solution.py:14
  14.5 9.0 %all-to-all-start = ((s32[8,1,2]{2,1,0:T(1,128)}), s32[8,1,2]{2,1,0:T(1,128)S(1)}, u32[]{:S(2)}, u32[]{:S(2)}) async-start(s32[8,1,2]{2,1,0:T(1,128)} %bitcast.7), calls=%async_computation | async-start | bytes 8192 | tf_op jit(solution)/shard_map/all_to_all | solution.py:40
  23.5 9.3 %reduce-scatter.6.cloned.1.call-done = f32[128,8,256]{0,2,1:T(8,128)} async-done(((f32[256,8,256]{0,2,1:T(8,128)}), f32[128,8,256]{0,2,1:T(8,128)}) %reduce-scatter.6.cloned.1.call-update) | async-done | bytes 1048592 | tf_op jit(solution)/shard_map/reduce_scatter | solution.py:13
  37.3 6.8 %all-to-all-start.1 = ((bf16[8,2,128,256]{3,1,2,0:T(2,128)(2,1)}), bf16[8,2,128,256]{3,1,2,0:T(2,128)(2,1)S(1)}, u32[]{:S(2)}, u32[]{:S(2)}) async-start(bf16[8,2,128,256]{3,1,2,0:T(2,128)(2,1)} %copy.30), calls=%async_computation.2 | async-start | bytes 2097152 | tf_op jit(solution)/shard_map/all_to_all | solution.py:37
  44.2 25.3 %all-gather = bf16[1,512,256]{2,1,0:T(8,128)(2,1)S(1)} all-gather(bf16[1,16,256]{2,1,0:T(8,128)(2,1)S(1)} %copy-done.1), channel_id=2, replica_groups=mesh['leaf'=16,'sep'=8,'mode'=2] {'leaf','mode'}, dimensions={1}, use_global_device_ids=true | all-gather | bytes 270336 | tf_op jit(solution)/shard_map/all_gather | solution.py:69
  70.8 2.6 all-to-all-done.1
  73.6 74.0 %while.26 = (s32[]{:T(128)}, f32[512,256]{1,0:T(8,128)S(1)}, s32[16]{0:T(128)S(1)}, bf16[16,128,256]{2,1,0:T(8,128)(2,1)S(1)}, bf16[512,256]{1,0:T(8,128)(2,1)S(1)}, /*index=5*/s32[]{:T(128)}, s32[]{:T(128)}, s32[]{:T(128)}) while((s32[]{:T(128)}, f32[512,256]{1,0:T(8,128)S(1)}, s32[16]{0:T(128)S(1)}, bf16[16,128,256]{2,1,0:T(8,128)(2,1)S(1)}, ...), condition=%wide.region_4.5_spmd, body=%wide.region_3.4_spmd.sunk | while | flops 33652740 | bytes 1312903 | solution.py:65
  80.6 1.9 dynamic_update_slice.16
  85.4 1.9 dynamic_update_slice.16
  90.2 1.9 dynamic_update_slice.16
  99.3 1.9 dynamic_update_slice.16
  127.4 1.9 dynamic_update_slice.16
  148.8 80.6 %reduce-scatter.8.cloned.1.call-done = f32[16,256]{1,0:T(8,128)} async-done(((f32[512,256]{1,0:T(8,128)}), f32[16,256]{1,0:T(8,128)}) %reduce-scatter.8.cloned.1.call-update) | async-done | bytes 16400 | tf_op jit(solution)/shard_map/reduce_scatter | solution.py:90
  230.1 30.9 %psum.28 = f32[256]{0:T(256)S(1)} all-reduce(f32[256]{0:T(256)S(1)} %multiply_reduce_fusion.1), channel_id=1, replica_groups=mesh['leaf'=16,'sep'=8,'mode'=2] {'leaf'}, use_global_device_ids=true, to_apply=%region_7.8 | all-reduce | flops 256 | bytes 2048 | tf_op jit(solution)/shard_map/psum | solution.py:96
  261.0 11.9 %psum.29 = f32[256]{0:T(256)S(1)} all-reduce(f32[256]{0:T(256)S(1)} %psum.28), channel_id=1, replica_groups=mesh['leaf'=16,'sep'=8,'mode'=2] {'mode'}, use_global_device_ids=true, to_apply=%region_8.9 | all-reduce | flops 256 | bytes 2048 | tf_op jit(solution)/shard_map/psum | solution.py:97
  273.8 22.1 %all_gather.7 = bf16[512,256]{1,0:T(8,128)(2,1)S(1)} all-gather(bf16[16,256]{1,0:T(8,128)(2,1)S(1)} %convolution_convert_fusion.4), channel_id=1, replica_groups=mesh['leaf'=16,'sep'=8,'mode'=2] {'leaf','mode'}, dimensions={0}, use_global_device_ids=true | all-gather | bytes 270336 | tf_op jit(solution)/shard_map/all_gather | solution.py:69
  296.0 85.1 %while.27 = (s32[]{:T(128)}, f32[512,256]{0,1:T(8,128)S(1)}, s32[16]{0:T(128)S(1)}, bf16[16,128,256]{2,1,0:T(8,128)(2,1)S(1)}, bf16[512,256]{1,0:T(8,128)(2,1)S(1)}, /*index=5*/s32[]{:T(128)}, s32[]{:T(128)}, s32[]{:T(128)}) while((s32[]{:T(128)}, f32[512,256]{0,1:T(8,128)S(1)}, s32[16]{0:T(128)S(1)}, bf16[16,128,256]{2,1,0:T(8,128)(2,1)S(1)}, ...), condition=%wide.region_10.11_spmd, body=%wide.region_9.10_spmd.sunk | while | flops 33652740 | bytes 2884751 | solution.py:65
  304.5 1.9 dynamic_update_slice.17
  309.8 1.9 dynamic_update_slice.17
  315.1 1.9 dynamic_update_slice.17
  325.5 1.9 dynamic_update_slice.17
  330.8 2.2 dynamic_update_slice.17
  336.4 1.9 dynamic_update_slice.17
  346.9 1.9 dynamic_update_slice.17
  352.2 2.2 dynamic_update_slice.17
  357.8 1.9 dynamic_update_slice.17
  368.2 1.9 dynamic_update_slice.17
  373.5 2.2 dynamic_update_slice.17
  379.1 1.9 dynamic_update_slice.17
  382.3 82.6 %reduce-scatter.10.cloned.1.call-done = f32[16,256]{1,0:T(8,128)} async-done(((f32[512,256]{1,0:T(8,128)}), f32[16,256]{1,0:T(8,128)}) %reduce-scatter.10.cloned.1.call-update) | async-done | bytes 16400
  465.9 30.9 %psum.30 = f32[256]{0:T(256)S(1)} all-reduce(f32[256]{0:T(256)S(1)} %multiply_reduce_fusion), channel_id=1, replica_groups=mesh['leaf'=16,'sep'=8,'mode'=2] {'leaf'}, use_global_device_ids=true, to_apply=%region_13.14 | all-reduce | flops 256 | bytes 2048 | tf_op jit(solution)/shard_map/psum | solution.py:96
  496.8 11.9 %psum.31 = f32[256]{0:T(256)S(1)} all-reduce(f32[256]{0:T(256)S(1)} %psum.30), channel_id=1, replica_groups=mesh['leaf'=16,'sep'=8,'mode'=2] {'mode'}, use_global_device_ids=true, to_apply=%region_14.15 | all-reduce | flops 256 | bytes 2048 | tf_op jit(solution)/shard_map/psum | solution.py:97
  (173 shorter events, 75.6 us)
Async XLA Ops:
  7.2 140.5 %copy-start = (bf16[1,512,16]{1,2,0:T(8,128)(2,1)S(1)}, bf16[1,512,16]{1,2,0:T(8,128)(2,1)}, u32[]{:S(2)}) copy-start(bf16[1,512,16]{1,2,0:T(8,128)(2,1)} %param.17) | copy-start | bytes 49156
  7.2 6.3 %copy-start.4 = (s32[8,1]{0,1:T(1,128)S(1)}, s32[8,1]{0,1:T(1,128)}, u32[]{:S(2)}) copy-start(s32[8,1]{0,1:T(1,128)} %param.15) | copy-start | bytes 100
  7.2 6.5 %copy-start.5 = (s32[8]{0:T(128)S(1)}, s32[8]{0:T(128)}, u32[]{:S(2)}) copy-start(s32[8]{0:T(128)} %param.16) | copy-start | bytes 100
  7.2 16.3 %copy-start.2 = (f32[8,128]{1,0:T(8,128)S(1)}, f32[8,128]{1,0:T(8,128)}, u32[]{:S(2)}) copy-start(f32[8,128]{1,0:T(8,128)} %param.14) | copy-start | bytes 12292
  7.2 25.6 %reduce-scatter.6.cloned.1.call-start = ((), (), s32[]{:S(2)}) async-start(), calls=%async_computation.5 | async-start | bytes 3145728 | tf_op jit(solution)/shard_map/reduce_scatter | solution.py:13
  14.5 22.9 %all-to-all-start = ((s32[8,1,2]{2,1,0:T(1,128)}), s32[8,1,2]{2,1,0:T(1,128)S(1)}, u32[]{:S(2)}, u32[]{:S(2)}) async-start(s32[8,1,2]{2,1,0:T(1,128)} %bitcast.7), calls=%async_computation | async-start | bytes 8192 | tf_op jit(solution)/shard_map/all_to_all | solution.py:40
  34.5 9.6 %copy-start.1 = (bf16[1,16,256]{2,1,0:T(8,128)(2,1)S(1)}, bf16[1,16,256]{2,1,0:T(8,128)(2,1)}, u32[]{:S(2)}) copy-start(bf16[1,16,256]{2,1,0:T(8,128)(2,1)} %param.18) | copy-start | bytes 24580
  37.3 36.0 %all-to-all-start.1 = ((bf16[8,2,128,256]{3,1,2,0:T(2,128)(2,1)}), bf16[8,2,128,256]{3,1,2,0:T(2,128)(2,1)S(1)}, u32[]{:S(2)}, u32[]{:S(2)}) async-start(bf16[8,2,128,256]{3,1,2,0:T(2,128)(2,1)} %copy.30), calls=%async_computation.2 | async-start | bytes 2097152 | tf_op jit(solution)/shard_map/all_to_all | solution.py:37
  44.1 185.3 %reduce-scatter.8.cloned.1.call-start = ((), (), s32[]{:S(2)}) async-start(), calls=%async_computation.6 | async-start | bytes 540672 | tf_op jit(solution)/shard_map/reduce_scatter | solution.py:90
  73.6 199.3 %copy-start.3 = (bf16[1,2,256,256]{3,2,1,0:T(8,128)(2,1)S(1)}, bf16[1,2,256,256]{3,2,1,0:T(8,128)(2,1)}, u32[]{:S(2)}) copy-start(bf16[1,2,256,256]{3,2,1,0:T(8,128)(2,1)} %param.19) | copy-start | bytes 786436
  148.7 316.2 %reduce-scatter.10.cloned.1.call-start = ((), (), s32[]{:S(2)}) async-start(), calls=%async_computation.7 | async-start | bytes 540672
Sparse Core Ops, SparseCore 0:
  13.6 19.1 reduce-scatter.5
  148.9 80.5 reduce-scatter.7
  382.5 82.4 reduce-scatter.9
